TPU v7x, 32 devices: a whole 2x2x4 slice. The times are simulated.
32 devices in a mesh: group: 2 (over y), patch: 4 (over z), head: 2 (over x), cfg: 2 (over core).
Axes of the slice: x: 2, y: 2, z: 4, core: 2. Of those that a mesh axis runs over, the one named last changes fastest.
Arguments:
- fresh_query: bfloat16 [4, 256, 2560], P(('group', 'cfg'), ('patch', 'head')), parts along dimension 0, may hold values from -32 to 32
- fresh_key: bfloat16 [4, 256, 2560], P(('group', 'cfg'), ('patch', 'head')), parts along dimension 0, may hold values from -9 to 9
- fresh_value: bfloat16 [4, 256, 2560], P(('group', 'cfg'), ('patch', 'head')), parts along dimension 0, may hold values from -12 to 12
- stale_key: bfloat16 [4, 256, 2560], P(('group', 'cfg'), 'patch', 'head'), parts along dimension 0, may hold values from -8 to 8
- stale_value: bfloat16 [4, 256, 2560], P(('group', 'cfg'), 'patch', 'head'), parts along dimension 0, may hold values from -12 to 12
- cross_query: bfloat16 [4, 256, 2560], P(('group', 'cfg'), ('patch', 'head')), parts along dimension 0, may hold values from -32 to 32
- text_key: bfloat16 [4, 512, 2560], P(('group', 'cfg'), None, 'head'), parts along dimension 0, may hold values from -8 to 8
- text_value: bfloat16 [4, 512, 2560], P(('group', 'cfg'), None, 'head'), parts along dimension 0, may hold values from -12 to 12
- text_mask: int32 [4, 512], P(('group', 'cfg')), parts along dimension 0, may hold values from 0 to 1, as said below
Outputs:
- self_mixed: bfloat16 [4, 256, 2560], P(('group', 'cfg'), ('patch', 'head')), parts along dimension 0
- cross_mixed: bfloat16 [4, 256, 2560], P(('group', 'cfg'), ('patch', 'head')), parts along dimension 0
There are 2 independent parts, one for each index of `group`. A program takes and returns all parts, laid end to end along the dimension named above; each array names one. Nothing has to cross between parts.
Inputs may be any that keep to these rules, and one draw needn't show every extreme that they name: In each branch the ones of text_mask form a prefix of 32 or more positions; in one of the two branches all 512 are ones, in the other some are zeros.
All inputs are finite; a program needn't handle non-finite values.
Results may differ from a plain program's by a relative error of at most 0.005.
Values may be sent and summed in bfloat16 or wider, within the bound.
A program may use at most 128 MiB of HBM per device.

v0:
```python
import math
import jax
import jax.numpy as jnp
from jax import lax
from jax.sharding import PartitionSpec as P

HD = 128


def scaled_scores(queries, key_block):
    return jnp.einsum("qhd,khd->qhk", queries, key_block, preferred_element_type=jnp.float32) * (
        1.0 / math.sqrt(HD)
    )


def absorb(running, scores, value_block, keeper):
    run_top, run_total, run_sum = running
    if keeper is None:
        piece_top = jnp.max(scores, axis=-1, keepdims=True)
        new_top = piece_top
        weights = jnp.exp(scores - new_top)
    else:
        piece_top = jnp.max(jnp.where(keeper, scores, -jnp.inf), axis=-1, keepdims=True)
        new_top = jnp.maximum(run_top, piece_top)
        weights = jnp.where(keeper, jnp.exp(jnp.where(keeper, scores, new_top) - new_top), 0.0)
    factor = jnp.exp(run_top - new_top)
    run_total = run_total * factor + jnp.sum(weights, axis=-1, keepdims=True)
    run_sum = run_sum * factor + jnp.einsum(
        "qhk,khd->qhd",
        weights.astype(jnp.bfloat16),
        value_block,
        preferred_element_type=jnp.float32,
    )
    return (new_top, run_total, run_sum)


def masked_mix(queries, key_block, value_block, usable):
    scores = scaled_scores(queries, key_block)
    row_top = jnp.max(jnp.where(usable, scores, -jnp.inf), axis=-1, keepdims=True)
    weights = jnp.where(usable, jnp.exp(jnp.where(usable, scores, row_top) - row_top), 0.0)
    totals = jnp.sum(weights, axis=-1, keepdims=True)
    mixture = jnp.einsum(
        "qhk,khd->qhd",
        weights.astype(jnp.bfloat16),
        value_block,
        preferred_element_type=jnp.float32,
    )
    return mixture / totals


def per_device(
    fresh_query,
    fresh_key,
    fresh_value,
    stale_key,
    stale_value,
    cross_query,
    text_key,
    text_value,
    text_mask,
):
    usable = (text_mask[0] > 0)[None, None, :]
    text_rows = text_key.shape[1]
    token_rows = fresh_query.shape[1]
    local_query, local_key, local_value = (
        lax.all_to_all(fresh_query, "head", split_axis=2, concat_axis=1, tiled=True),
        lax.all_to_all(fresh_key, "head", split_axis=2, concat_axis=1, tiled=True),
        lax.all_to_all(fresh_value, "head", split_axis=2, concat_axis=1, tiled=True),
    )
    patch_rows = local_query.shape[1]
    heads_here = local_query.shape[2] // HD
    queries = local_query.reshape(patch_rows, heads_here, HD)
    own_keys = local_key.reshape(patch_rows, heads_here, HD)
    own_values = local_value.reshape(patch_rows, heads_here, HD)
    own_first = lax.axis_index("patch") * patch_rows
    starting = (
        jnp.full((patch_rows, heads_here, 1), -jnp.inf, jnp.float32),
        jnp.zeros((patch_rows, heads_here, 1), jnp.float32),
        jnp.zeros((patch_rows, heads_here, HD), jnp.float32),
    )
    opening = absorb(starting, scaled_scores(queries, own_keys), own_values, None)
    piece_key = lax.all_gather(stale_key, "patch", axis=1, tiled=True)
    piece_value = lax.all_gather(stale_value, "patch", axis=1, tiled=True)
    row_count = piece_key.shape[1]
    keys_here = piece_key.reshape(row_count, heads_here, HD)
    values_here = piece_value.reshape(row_count, heads_here, HD)
    positions = jnp.arange(row_count, dtype=jnp.int32)
    keeper = ((positions < own_first) | (positions >= own_first + patch_rows))[None, None, :]
    run_top, run_total, run_sum = absorb(
        opening, scaled_scores(queries, keys_here), values_here, keeper
    )
    self_block = (run_sum / run_total).reshape(1, patch_rows, heads_here * HD).astype(jnp.bfloat16)
    all_heads = cross_query.shape[2] // HD
    cross_heads = cross_query.reshape(token_rows, all_heads, HD)
    piece_key, piece_value = lax.all_gather(
        (
            text_key.reshape(1, text_rows, heads_here, HD),
            text_value.reshape(1, text_rows, heads_here, HD),
        ),
        "head",
        axis=2,
        tiled=True,
    )
    mixture = masked_mix(cross_heads, piece_key[0], piece_value[0], usable)
    gathered = mixture.astype(jnp.bfloat16)[None]
    cross_block = gathered.reshape(1, token_rows, all_heads * HD)
    self_mixed = lax.all_to_all(self_block, "head", split_axis=1, concat_axis=2, tiled=True)
    return (self_mixed, cross_block)


def solution(mesh):
    return jax.shard_map(
        per_device,
        mesh=mesh,
        in_specs=(
            P(("group", "cfg"), ("patch", "head"), None),
            P(("group", "cfg"), ("patch", "head"), None),
            P(("group", "cfg"), ("patch", "head"), None),
            P(("group", "cfg"), "patch", "head"),
            P(("group", "cfg"), "patch", "head"),
            P(("group", "cfg"), ("patch", "head"), None),
            P(("group", "cfg"), None, "head"),
            P(("group", "cfg"), None, "head"),
            P(("group", "cfg"), None),
        ),
        out_specs=(
            P(("group", "cfg"), ("patch", "head"), None),
            P(("group", "cfg"), ("patch", "head"), None),
        ),
        check_vma=False,
    )
```

profile of v0, /device:TPU:0, one launch (start us, length us, event | category | flops | bytes accessed | tf_op | source)
XLA Modules:
  0.0 149.4 jit_solution(1958415783337173645)
XLA Ops:
  7.2 0.0 all-gather.3.cloned.1.call-start
  7.2 1.6 %copy.97 = bf16[1,512,1280]{1,2,0:T(8,128)(2,1)S(1)} copy(bf16[1,512,1280]{2,1,0:T(8,128)(2,1)} %param.15) | data formatting | bytes 2621440 | tf_op args[6]
  8.8 1.5 copy.98
  10.3 0.0 all-gather.3.cloned.1.call-update
  10.3 0.9 copy-done.5
  11.2 0.9 copy.79
  12.1 0.6 broadcast.39
  12.7 14.4 %reduce.2 = bf16[2560,32]{1,0:T(8,128)(2,1)S(1)} reduce(bf16[2560,1,32]{2,1,0:T(2,128)(2,1)S(1)} %bitcast.72, bf16[]{:T(256)} %broadcast.39), dimensions={1}, to_apply=%bitcast.62.reduce_sub_computation | reduce | bytes 327682
  27.1 1.3 reshape.109
  28.4 4.2 %all-to-all-start.1 = ((bf16[2,2,20480]{2,1,0:T(2,128)(2,1)}), bf16[2,2,20480]{2,1,0:T(2,128)(2,1)S(1)}, u32[]{:S(2)}, u32[]{:S(2)}) async-start(bf16[2,2,20480]{2,1,0:T(2,128)(2,1)} %reshape.109), calls=%async_computation.1 | async-start | bytes 327680 | tf_op jit(solution)/shard_map/all_to_all | solution.py:66
  32.7 0.6 copy.100
  33.3 1.4 copy.101
  34.8 0.0 all-gather.5.cloned.1.call-update
  34.8 0.9 copy-done.3
  35.7 19.2 %all_gather.12 = bf16[1,256,1280]{2,1,0:T(8,128)(2,1)S(1)} all-gather(bf16[1,64,1280]{2,1,0:T(8,128)(2,1)S(1)} %copy-done.3), channel_id=1, replica_groups=mesh['group'=2,'patch'=4,'head'=2,'cfg'=2] {'patch'}, dimensions={1}, use_global_device_ids=true | all-gather | bytes 819200 | tf_op jit(solution)/shard_map/all_gather | solution.py:82
  54.8 0.9 copy.76
  55.8 0.0 copy-start.4
  55.8 14.3 %reduce.3 = bf16[2560,32]{1,0:T(8,128)(2,1)S(1)} reduce(bf16[2560,1,32]{2,1,0:T(2,128)(2,1)S(1)} %bitcast.78, bf16[]{:T(256)} %broadcast.39), dimensions={1}, to_apply=%bitcast.60.reduce_sub_computation | reduce | bytes 327682
  70.1 0.0 copy-start.2
  70.1 1.3 reshape.107
  71.4 0.0 all-to-all-done.1
  71.4 4.1 %all-to-all-start = ((bf16[2,2,20480]{2,1,0:T(2,128)(2,1)}), bf16[2,2,20480]{2,1,0:T(2,128)(2,1)}, u32[]{:S(2)}, u32[]{:S(2)}) async-start(bf16[2,2,20480]{2,1,0:T(2,128)(2,1)} %reshape.107), calls=%async_computation | async-start | bytes 327680 | tf_op jit(solution)/shard_map/all_to_all | solution.py:67
  75.5 16.1 %all_gather.13 = bf16[1,256,1280]{2,1,0:T(8,128)(2,1)S(1)} all-gather(bf16[1,64,1280]{2,1,0:T(8,128)(2,1)S(1)} %copy-done.4), channel_id=1, replica_groups=mesh['group'=2,'patch'=4,'head'=2,'cfg'=2] {'patch'}, dimensions={1}, use_global_device_ids=true | all-gather | bytes 819200 | tf_op jit(solution)/shard_map/all_gather | solution.py:83
  91.6 0.1 reshape.104
  91.7 0.2 copy.89
  92.0 0.0 copy-start.7
  92.0 0.2 copy.92
  92.2 0.7 copy-done.7
  92.9 0.9 copy.84
  93.8 14.3 %reduce.4 = bf16[2560,32]{1,0:T(8,128)(2,1)S(1)} reduce(bf16[2560,1,32]{2,1,0:T(2,128)(2,1)S(1)} %bitcast.79, bf16[]{:T(256)} %broadcast.39), dimensions={1}, to_apply=%bitcast.64.reduce_sub_computation | reduce | bytes 327682
  108.1 1.3 reshape.111
  109.4 0.0 all-to-all-done
  109.4 4.3 %all-to-all-start.2 = ((bf16[2,2,20480]{2,1,0:T(2,128)(2,1)}), bf16[2,2,20480]{2,1,0:T(2,128)(2,1)}, u32[]{:S(2)}, u32[]{:S(2)}) async-start(bf16[2,2,20480]{2,1,0:T(2,128)(2,1)} %reshape.111), calls=%async_computation.2 | async-start | bytes 327680 | tf_op jit(solution)/shard_map/all_to_all | solution.py:68
  113.8 1.5 reshape.110
  115.2 0.7 copy.80
  116.0 0.1 reshape.99
  116.2 1.5 reshape.108
  117.6 0.7 copy.77
  118.4 0.1 reshape.98
  118.5 0.0 all-to-all-done.2
  118.6 1.5 reshape.112
  120.1 1.7 %copy.85 = bf16[1,32,2560]{2,1,0:T(8,128)(2,1)} copy(bf16[1,32,2560]{1,0,2:T(2,128)(2,1)S(1)} %bitcast.75) | data formatting | bytes 327680 | tf_op jit(solution)/shard_map/all_to_all | solution.py:68
  121.8 1.0 all_to_all.53
  122.8 0.1 reshape.100
  122.9 0.2 fusion.49
  123.1 0.3 select_reduce_fusion.1
  123.5 0.1 fusion.38
  123.6 0.3 fusion.32
  123.9 0.3 fusion.17
  124.2 0.4 fusion.22
  124.6 0.1 copy.94
  124.8 0.1 convert_element_type.32
  124.9 1.6 %reduce.5 = bf16[64,1280]{1,0:T(8,128)(2,1)S(1)} reduce(bf16[64,1,1280]{2,1,0:T(2,128)(2,1)S(1)} %bitcast.81, bf16[]{:T(256)} %broadcast.39), dimensions={1}, to_apply=%bitcast.66.reduce_sub_computation | reduce | bytes 327682
  126.5 0.7 reshape.113
  127.2 3.4 %all-to-all-start.3 = ((bf16[2,2,20480]{2,1,0:T(2,128)(2,1)}), bf16[2,2,20480]{2,1,0:T(2,128)(2,1)S(1)}, u32[]{:S(2)}, u32[]{:S(2)}) async-start(bf16[2,2,20480]{2,1,0:T(2,128)(2,1)} %reshape.113), calls=%async_computation.3 | async-start | bytes 327680 | tf_op jit(solution)/shard_map/all_to_all | solution.py:107
  130.7 4.6 %all-to-all-done.3 = bf16[2,2,20480]{2,1,0:T(2,128)(2,1)S(1)} async-done(((bf16[2,2,20480]{2,1,0:T(2,128)(2,1)}), bf16[2,2,20480]{2,1,0:T(2,128)(2,1)S(1)}, u32[]{:S(2)}, u32[]{:S(2)}) %all-to-all-start.3) | async-done | bytes 163872 | tf_op jit(solution)/shard_map/all_to_all | solution.py:107
  135.3 0.2 reshape.114
  135.4 0.7 copy.107
  136.1 2.8 %select_reduce_fusion = (f32[32,20]{0,1:T(8,128)S(1)}, f32[32,20,512]{2,0,1:T(8,128)S(1)}) fusion(pred[512]{0:T(512)(128)(4,1)S(1)} %compare_reduce_fusion, bf16[32,20,128]{2,1,0:T(8,128)(2,1)S(1)} %reshape.104, bf16[1,512,20,128]{3,1,0,2:T(8,128)(2,1)} %all-gather.3.cloned.1.call-done), kind=kOutput, calls=%fused_computation.7 | convolution fusion | flops 84868480 | bytes 4099072 | tf_op jit(solution)/shard_map/qhd,khd->qhk/dot_general | solution.py:11
  138.9 0.4 fusion.26
  139.4 0.0 all-gather.5.cloned.1.call-done
  139.4 2.3 %fusion.23 = bf16[32,20,128]{2,0,1:T(8,128)(2,1)S(1)} fusion(bf16[1,512,20,128]{3,1,0,2:T(8,128)(2,1)} %all-gather.5.cloned.1.call-done, f32[32,20,512]{2,0,1:T(8,128)S(1)} %get-tuple-element.10, f32[32,20]{0,1:T(8,128)S(1)} %get-tuple-element.9, pred[512]{0:T(512)(128)(4,1)S(1)} %compare_reduce_fusion, f32[32,20]{0,1:T(8,128)S(1)} %fusion.26), kind=kOutput, calls=%fused_computation.21 | convolution fusion | flops 85360640 | bytes 4101632 | tf_op jit(solution)/shard_map/qhk,khd->qhd/dot_general | solution.py:42
  141.7 0.1 copy.102
  141.8 0.8 reshape_broadcast_in_dim.3
  (24 shorter events, 0.2 us)
Async XLA Ops:
  7.2 129.0 %all-gather.3.cloned.1.call-start = ((), (), s32[]{:S(2)}) async-start(), calls=%async_computation.4 | async-start | bytes 3932160 | tf_op jit(solution)/shard_map/all_gather | solution.py:95
  10.3 0.9 copy-start.5
  12.7 20.0 %copy-start = (bf16[1,512,1280]{2,1,0:T(8,128)(2,1)S(1)}, bf16[1,512,1280]{2,1,0:T(8,128)(2,1)}, u32[]{:S(2)}) copy-start(bf16[1,512,1280]{2,1,0:T(8,128)(2,1)} %param.16) | copy-start | bytes 3932164
  28.4 43.0 %all-to-all-start.1 = ((bf16[2,2,20480]{2,1,0:T(2,128)(2,1)}), bf16[2,2,20480]{2,1,0:T(2,128)(2,1)S(1)}, u32[]{:S(2)}, u32[]{:S(2)}) async-start(bf16[2,2,20480]{2,1,0:T(2,128)(2,1)} %reshape.109), calls=%async_computation.1 | async-start | bytes 327680 | tf_op jit(solution)/shard_map/all_to_all | solution.py:66
  32.7 106.7 %all-gather.5.cloned.1.call-start = ((), (), s32[]{:S(2)}) async-start(), calls=%async_computation.5 | async-start | bytes 3932160 | tf_op jit(solution)/shard_map/all_gather | solution.py:95
  34.8 0.9 copy-start.3
  34.8 20.1 %copy-start.6 = (bf16[1,32,2560]{2,1,0:T(8,128)(2,1)S(1)}, bf16[1,32,2560]{2,1,0:T(8,128)(2,1)}, u32[]{:S(2)}) copy-start(bf16[1,32,2560]{2,1,0:T(8,128)(2,1)} %param.10) | copy-start | bytes 491524
  55.8 19.7 %copy-start.4 = (bf16[1,64,1280]{2,1,0:T(8,128)(2,1)S(1)}, bf16[1,64,1280]{2,1,0:T(8,128)(2,1)}, u32[]{:S(2)}) copy-start(bf16[1,64,1280]{2,1,0:T(8,128)(2,1)} %param.13) | copy-start | bytes 491524
  70.1 21.5 %copy-start.2 = (bf16[1,32,2560]{2,1,0:T(8,128)(2,1)S(1)}, bf16[1,32,2560]{2,1,0:T(8,128)(2,1)}, u32[]{:S(2)}) copy-start(bf16[1,32,2560]{2,1,0:T(8,128)(2,1)} %param.14) | copy-start | bytes 491524
  71.4 20.3 %copy-start.1 = (bf16[2,2,20480]{2,1,0:T(2,128)(2,1)}, bf16[2,2,20480]{2,1,0:T(2,128)(2,1)S(1)}, u32[]{:S(2)}) copy-start(bf16[2,2,20480]{2,1,0:T(2,128)(2,1)S(1)} %all-to-all-done.1) | copy-start | bytes 491524
  71.4 38.0 %all-to-all-start = ((bf16[2,2,20480]{2,1,0:T(2,128)(2,1)}), bf16[2,2,20480]{2,1,0:T(2,128)(2,1)}, u32[]{:S(2)}, u32[]{:S(2)}) async-start(bf16[2,2,20480]{2,1,0:T(2,128)(2,1)} %reshape.107), calls=%async_computation | async-start | bytes 327680 | tf_op jit(solution)/shard_map/all_to_all | solution.py:67
  92.0 0.9 copy-start.7
  109.4 9.1 %all-to-all-start.2 = ((bf16[2,2,20480]{2,1,0:T(2,128)(2,1)}), bf16[2,2,20480]{2,1,0:T(2,128)(2,1)}, u32[]{:S(2)}, u32[]{:S(2)}) async-start(bf16[2,2,20480]{2,1,0:T(2,128)(2,1)} %reshape.111), calls=%async_computation.2 | async-start | bytes 327680 | tf_op jit(solution)/shard_map/all_to_all | solution.py:68
  124.6 6.0 %copy-start.8 = (s32[1,512]{1,0:T(1,128)S(1)}, s32[1,512]{1,0:T(1,128)}, u32[]{:S(2)}) copy-start(s32[1,512]{1,0:T(1,128)} %param.17) | copy-start | bytes 6148
  127.2 8.1 %all-to-all-start.3 = ((bf16[2,2,20480]{2,1,0:T(2,128)(2,1)}), bf16[2,2,20480]{2,1,0:T(2,128)(2,1)S(1)}, u32[]{:S(2)}, u32[]{:S(2)}) async-start(bf16[2,2,20480]{2,1,0:T(2,128)(2,1)} %reshape.113), calls=%async_computation.3 | async-start | bytes 327680 | tf_op jit(solution)/shard_map/all_to_all | solution.py:107
Sparse Core Ops, SparseCore 0:
  10.4 43.4 all-gather.2
  55.5 40.7 all-gather.4
where the time goes:
time: 150 us; the launch traced here: 149 us
  other arithmetic  45.5 us (30%)
  blocking collectives  35.3 us (24%)
  local copies, waits for them, and re-layouts  27.1 us (18%)
  starting transfers between devices  16 us (11%)
  between operations  14.4 us (10%)
  matrix products  6.43 us (4%)
  waiting for transfers between devices  4.66 us (3%)
    unnamed x4, other arithmetic  44.7 us
    all_gather x1, blocking collectives, per_device(): piece_key = lax.all_gather(stale_key, 'patch', axis=1, tiled=True)  19.2 us
    unnamed x33, local copies, waits for them, and re-layouts  17.3 us
    all_gather x1, blocking collectives, per_device(): piece_value = lax.all_gather(stale_value, 'patch', axis=1, tiled=True)  16.1 us
    all_to_all x1, waiting for transfers between devices, per_device(): lax.all_to_all(self_block, 'head', split_axis=1, concat_axis=2, tiled=True)  4.6 us
    all_to_all x1, starting transfers between devices, per_device(): lax.all_to_all(fresh_value, 'head', split_axis=2, concat_axis=1, tiled=True)  4.28 us
    all_to_all x1, starting transfers between devices, per_device(): lax.all_to_all(fresh_query, 'head', split_axis=2, concat_axis=1, tiled=True)  4.23 us
    all_to_all x1, starting transfers between devices, per_device(): lax.all_to_all(fresh_key, 'head', split_axis=2, concat_axis=1, tiled=True)  4.05 us
  transfers between devices with their start and end apart: 6, of which 1 were waited for; matrix products, arithmetic and copies ran while one was open for 46% of the time, Pallas kernels for 0%

commit v1 on v0

--- a/solution.py
+++ b/solution.py
@@ -5,6 +5,12 @@
 from jax.sharding import PartitionSpec as P
 
 HD = 128
+
+
+def in_order(tiles, dim):
+    tiles = jnp.moveaxis(tiles, 0, dim)
+    shape = tiles.shape
+    return tiles.reshape(*shape[:dim], shape[dim] * shape[dim + 1], *shape[dim + 2 :])
 
 
 def scaled_scores(queries, key_block):
@@ -80,7 +86,19 @@
     )
     opening = absorb(starting, scaled_scores(queries, own_keys), own_values, None)
     piece_key = lax.all_gather(stale_key, "patch", axis=1, tiled=True)
-    piece_value = lax.all_gather(stale_value, "patch", axis=1, tiled=True)
+    size = lax.axis_size("patch")
+    pairs = [(i, (i + 1) % size) for i in range(size)]
+    back = [(b, a) for a, b in pairs]
+    lower, upper = ([], [])
+    for step in range(size - 1):
+        if step % 2 == 0:
+            lower.append(lax.ppermute(lower[-1] if lower else stale_value, "patch", pairs))
+        else:
+            upper.append(lax.ppermute(upper[-1] if upper else stale_value, "patch", back))
+    blocks = jnp.stack([*lower[::-1], stale_value, *upper])
+    shift = lax.axis_index("patch") - len(lower)
+    blocks = blocks[(jnp.arange(size) - shift) % size]
+    piece_value = in_order(blocks, 1)
     row_count = piece_key.shape[1]
     keys_here = piece_key.reshape(row_count, heads_here, HD)
     values_here = piece_value.reshape(row_count, heads_here, HD)

time: 150 us -> 144 us (0.960)
  blocking collectives: 35.3 us -> 16.6 us
  waiting for transfers between devices: 4.66 us -> 17.6 us
  local copies, waits for them, and re-layouts: 27.1 us -> 22 us
  starting transfers between devices: 16 us -> 19.3 us
    all_gather x1 -> x0, blocking collectives: 16.1 us -> none  [per_device(): piece_value = lax.all_gather(stale_value, 'patch', axis=1, tiled=True)]
    ppermute x0 -> x3, waiting for transfers between devices: none -> 6.98 us  [the longest x2 6.98 us: per_device(): lax.ppermute(lower[-1] if lower else stale_value, 'patch', pairs)]
    ppermute x0 -> x3, starting transfers between devices: none -> 5.26 us  [the longest x2 3.16 us: per_device(): lax.ppermute(lower[-1] if lower else stale_value, 'patch', pairs)]
    all_to_all x1, waiting for transfers between devices: 0.01 us -> 4.62 us  [per_device(): lax.all_to_all(fresh_key, 'head', split_axis=2, concat_axis=1, tiled=True)]
    unnamed x33, local copies, waits for them, and re-layouts: 17.3 us -> 13.4 us
    all_gather x1, blocking collectives: 19.2 us -> 16.6 us  [per_device(): piece_key = lax.all_gather(stale_key, 'patch', axis=1, tiled=True)]
    all_to_all x3, local copies, waits for them, and re-layouts: 2.72 us -> 0.77 us  [per_device(): lax.all_to_all(fresh_value, 'head', split_axis=2, concat_axis=1, tiled=True)]
  transfers between devices with their start and end apart: 6 -> 9, of which waited for: 1 -> 4; matrix products, arithmetic and copies ran while one was open for 46% -> 47% of each run, Pallas kernels for 0% -> 0%
where the time goes in v1:
time: 144 us; the launch traced here: 143 us
  other arithmetic  46.7 us (32%)
  local copies, waits for them, and re-layouts  22 us (15%)
  starting transfers between devices  19.3 us (13%)
  waiting for transfers between devices  17.6 us (12%)
  blocking collectives  16.6 us (12%)
  between operations  14.5 us (10%)
  matrix products  6.39 us (4%)
    unnamed x4, other arithmetic  44.7 us
    all_gather x1, blocking collectives, per_device(): piece_key = lax.all_gather(stale_key, 'patch', axis=1, tiled=True)  16.6 us
    unnamed x33, local copies, waits for them, and re-layouts  13.4 us
    ppermute x2, waiting for transfers between devices, per_device(): lax.ppermute(lower[-1] if lower else stale_value, 'patch', pairs)  6.98 us
    all_to_all x1, waiting for transfers between devices, per_device(): lax.all_to_all(fresh_key, 'head', split_axis=2, concat_axis=1, tiled=True)  4.62 us
    all_to_all x1, waiting for transfers between devices, per_device(): lax.all_to_all(self_block, 'head', split_axis=1, concat_axis=2, tiled=True)  4.6 us
    all_to_all x1, starting transfers between devices, per_device(): lax.all_to_all(fresh_value, 'head', split_axis=2, concat_axis=1, tiled=True)  3.65 us
    all_to_all x1, starting transfers between devices, per_device(): lax.all_to_all(fresh_key, 'head', split_axis=2, concat_axis=1, tiled=True)  3.44 us
  transfers between devices with their start and end apart: 9, of which 4 were waited for; matrix products, arithmetic and copies ran while one was open for 47% of the time, Pallas kernels for 0%

profile of v1, /device:TPU:0, one launch (start us, length us, event | category | flops | bytes accessed | tf_op | source)
XLA Modules:
  0.0 143.1 jit_solution(11603193958656270131)
XLA Ops:
  7.2 0.0 all-gather.3.cloned.1.call-start
  7.2 1.6 %copy.94 = bf16[1,512,1280]{1,2,0:T(8,128)(2,1)S(1)} copy(bf16[1,512,1280]{2,1,0:T(8,128)(2,1)} %param.15) | data formatting | bytes 2621440 | tf_op args[6]
  8.8 1.5 %copy.95 = bf16[1,512,10,128]{3,1,0,2:T(8,128)(2,1)} copy(bf16[1,512,10,128]{1,3,2,0:T(8,128)(2,1)S(1)} %bitcast.82) | data formatting | bytes 2621440 | tf_op jit(solution)/shard_map/reshape | solution.py:115
  10.3 0.0 all-gather.3.cloned.1.call-update
  10.3 3.1 %collective-permute-start = (bf16[1,64,1280]{2,1,0:T(8,128)(2,1)}, bf16[1,64,1280]{2,1,0:T(8,128)(2,1)}, u32[]{:S(2)}, u32[]{:S(2)}) collective-permute-start(bf16[1,64,1280]{2,1,0:T(8,128)(2,1)} %param.13), channel_id=1, source_target_pairs={{0,4},{4,8},{8,12},{12,0},{1,5},{5,9},{9,13},{13,1},{2,6},{6,10},{... | collective-permute-start | bytes 491528 | tf_op jit(solution)/shard_map/ppermute | solution.py:95
  13.4 2.1 %collective-permute-start.2 = (bf16[1,64,1280]{2,1,0:T(8,128)(2,1)}, bf16[1,64,1280]{2,1,0:T(8,128)(2,1)}, u32[]{:S(2)}, u32[]{:S(2)}) collective-permute-start(bf16[1,64,1280]{2,1,0:T(8,128)(2,1)} %param.13), channel_id=1, source_target_pairs={{4,0},{8,4},{12,8},{0,12},{5,1},{9,5},{13,9},{1,13},{6,2},{10,6},{... | collective-permute-start | bytes 491528 | tf_op jit(solution)/shard_map/ppermute | solution.py:97
  15.5 0.9 copy.77
  16.4 0.6 broadcast.108
  17.0 14.4 %reduce.2 = bf16[2560,32]{1,0:T(8,128)(2,1)S(1)} reduce(bf16[2560,1,32]{2,1,0:T(2,128)(2,1)S(1)} %bitcast.78, bf16[]{:T(256)} %broadcast.108), dimensions={1}, to_apply=%bitcast.69.reduce_sub_computation | reduce | bytes 327682
  31.4 1.3 reshape.165
  32.7 3.4 %all-to-all-start.1 = ((bf16[2,2,20480]{2,1,0:T(2,128)(2,1)}), bf16[2,2,20480]{2,1,0:T(2,128)(2,1)S(1)}, u32[]{:S(2)}, u32[]{:S(2)}) async-start(bf16[2,2,20480]{2,1,0:T(2,128)(2,1)} %reshape.165), calls=%async_computation.1 | async-start | bytes 327680 | tf_op jit(solution)/shard_map/all_to_all | solution.py:72
  36.2 0.0 all-gather.5.cloned.1.call-start
  36.2 0.7 copy.97
  36.9 1.4 %copy.98 = bf16[1,512,10,128]{3,1,0,2:T(8,128)(2,1)} copy(bf16[1,512,10,128]{1,3,2,0:T(8,128)(2,1)S(1)} %bitcast.83) | data formatting | bytes 2621440 | tf_op jit(solution)/shard_map/reshape | solution.py:116
  38.3 0.0 all-gather.5.cloned.1.call-update
  38.4 0.9 copy-done.1
  39.2 0.1 reshape.149
  39.4 16.6 %all_gather.9 = bf16[1,256,1280]{2,1,0:T(8,128)(2,1)S(1)} all-gather(bf16[1,64,1280]{2,1,0:T(8,128)(2,1)S(1)} %copy-done.2), channel_id=1, replica_groups=mesh['group'=2,'patch'=4,'head'=2,'cfg'=2] {'patch'}, dimensions={1}, use_global_device_ids=true | all-gather | bytes 819200 | tf_op jit(solution)/shard_map/all_gather | solution.py:88
  56.0 0.2 copy.87
  56.3 0.9 copy.74
  57.2 14.3 %reduce.3 = bf16[2560,32]{1,0:T(8,128)(2,1)S(1)} reduce(bf16[2560,1,32]{2,1,0:T(2,128)(2,1)S(1)} %bitcast.84, bf16[]{:T(256)} %broadcast.108), dimensions={1}, to_apply=%bitcast.67.reduce_sub_computation | reduce | bytes 327682
  71.6 1.3 reshape.163
  72.9 0.9 copy.82
  73.8 14.3 %reduce.4 = bf16[2560,32]{1,0:T(8,128)(2,1)S(1)} reduce(bf16[2560,1,32]{2,1,0:T(2,128)(2,1)S(1)} %bitcast.85, bf16[]{:T(256)} %broadcast.108), dimensions={1}, to_apply=%bitcast.71.reduce_sub_computation | reduce | bytes 327682
  88.1 1.3 reshape.167
  89.4 3.4 %all-to-all-start = ((bf16[2,2,20480]{2,1,0:T(2,128)(2,1)}), bf16[2,2,20480]{2,1,0:T(2,128)(2,1)S(1)}, u32[]{:S(2)}, u32[]{:S(2)}) async-start(bf16[2,2,20480]{2,1,0:T(2,128)(2,1)} %reshape.163), calls=%async_computation | async-start | bytes 327680 | tf_op jit(solution)/shard_map/all_to_all | solution.py:73
  92.9 4.6 %all-to-all-done = bf16[2,2,20480]{2,1,0:T(2,128)(2,1)S(1)} async-done(((bf16[2,2,20480]{2,1,0:T(2,128)(2,1)}), bf16[2,2,20480]{2,1,0:T(2,128)(2,1)S(1)}, u32[]{:S(2)}, u32[]{:S(2)}) %all-to-all-start) | async-done | bytes 163872 | tf_op jit(solution)/shard_map/all_to_all | solution.py:73
  97.5 3.6 %all-to-all-start.2 = ((bf16[2,2,20480]{2,1,0:T(2,128)(2,1)}), bf16[2,2,20480]{2,1,0:T(2,128)(2,1)S(1)}, u32[]{:S(2)}, u32[]{:S(2)}) async-start(bf16[2,2,20480]{2,1,0:T(2,128)(2,1)} %reshape.167), calls=%async_computation.2 | async-start | bytes 327680 | tf_op jit(solution)/shard_map/all_to_all | solution.py:74
  101.2 0.6 reshape.166
  101.8 0.7 copy.78
  102.6 0.1 reshape.145
  102.7 0.6 reshape.164
  103.4 0.7 copy.75
  104.1 0.1 reshape.144
  104.3 1.3 all-to-all-done.2
  105.6 0.6 reshape.168
  106.2 0.7 copy.83
  107.0 0.1 reshape.146
  107.1 0.2 fusion.52
  107.3 0.3 select_reduce_fusion.1
  107.7 0.1 fusion.39
  107.8 0.3 fusion.33
  108.1 0.1 collective-permute-start.1
  108.2 0.3 fusion.17
  108.5 7.0 %collective-permute-done.1 = bf16[1,64,1280]{2,1,0:T(8,128)(2,1)S(1)} collective-permute-done((bf16[1,64,1280]{2,1,0:T(8,128)(2,1)}, bf16[1,64,1280]{2,1,0:T(8,128)(2,1)S(1)}, u32[]{:S(2)}, u32[]{:S(2)}) %collective-permute-start.1) | collective-permute-done | bytes 163872 | tf_op jit(solution)/shard_map/ppermute | solution.py:95
  115.5 1.2 maximum_bitcast_fusion
  116.6 0.6 gather_fusion
  117.2 0.4 reshape_reshape_transpose.3
  117.6 0.2 copy-done.7
  117.9 0.4 fusion.22
  118.3 0.1 copy.91
  118.4 0.1 convert_element_type.32
  118.5 1.6 %reduce.5 = bf16[64,1280]{1,0:T(8,128)(2,1)S(1)} reduce(bf16[64,1,1280]{2,1,0:T(2,128)(2,1)S(1)} %bitcast.87, bf16[]{:T(256)} %broadcast.108), dimensions={1}, to_apply=%bitcast.73.reduce_sub_computation | reduce | bytes 327682
  120.1 0.7 reshape.169
  120.8 3.4 %all-to-all-start.3 = ((bf16[2,2,20480]{2,1,0:T(2,128)(2,1)}), bf16[2,2,20480]{2,1,0:T(2,128)(2,1)S(1)}, u32[]{:S(2)}, u32[]{:S(2)}) async-start(bf16[2,2,20480]{2,1,0:T(2,128)(2,1)} %reshape.169), calls=%async_computation.3 | async-start | bytes 327680 | tf_op jit(solution)/shard_map/all_to_all | solution.py:125
  124.3 4.6 %all-to-all-done.3 = bf16[2,2,20480]{2,1,0:T(2,128)(2,1)S(1)} async-done(((bf16[2,2,20480]{2,1,0:T(2,128)(2,1)}), bf16[2,2,20480]{2,1,0:T(2,128)(2,1)S(1)}, u32[]{:S(2)}, u32[]{:S(2)}) %all-to-all-start.3) | async-done | bytes 163872 | tf_op jit(solution)/shard_map/all_to_all | solution.py:125
  128.9 0.2 reshape.170
  129.1 0.7 copy.103
  129.8 2.8 %select_reduce_fusion = (f32[32,20]{0,1:T(8,128)S(1)}, f32[32,20,512]{2,0,1:T(8,128)S(1)}) fusion(pred[512]{0:T(512)(128)(4,1)S(1)} %compare_reduce_fusion, bf16[32,20,128]{2,1,0:T(8,128)(2,1)S(1)} %reshape.149, bf16[1,512,20,128]{3,1,0,2:T(8,128)(2,1)} %all-gather.3.cloned.1.call-done), kind=kOutput, calls=%fused_computation.8 | convolution fusion | flops 84868480 | bytes 4099072 | tf_op jit(solution)/shard_map/qhd,khd->qhk/dot_general | solution.py:17
  132.6 0.4 fusion.26
  133.0 0.0 all-gather.5.cloned.1.call-done
  133.0 2.3 %fusion.23 = bf16[32,20,128]{2,0,1:T(8,128)(2,1)S(1)} fusion(bf16[1,512,20,128]{3,1,0,2:T(8,128)(2,1)} %all-gather.5.cloned.1.call-done, f32[32,20,512]{2,0,1:T(8,128)S(1)} %get-tuple-element.10, f32[32,20]{0,1:T(8,128)S(1)} %get-tuple-element.9, pred[512]{0:T(512)(128)(4,1)S(1)} %compare_reduce_fusion, f32[32,20]{0,1:T(8,128)S(1)} %fusion.26), kind=kOutput, calls=%fused_computation.22 | convolution fusion | flops 85360640 | bytes 4101632 | tf_op jit(solution)/shard_map/qhk,khd->qhd/dot_general | solution.py:48
  135.4 0.1 copy.99
  135.4 0.8 reshape_broadcast_in_dim.3
  (33 shorter events, 0.3 us)
Async XLA Ops:
  7.2 122.6 %all-gather.3.cloned.1.call-start = ((), (), s32[]{:S(2)}) async-start(), calls=%async_computation.4 | async-start | bytes 3932160 | tf_op jit(solution)/shard_map/all_gather | solution.py:113
  10.3 5.2 %copy-start.3 = (bf16[1,32,2560]{2,1,0:T(8,128)(2,1)S(1)}, bf16[1,32,2560]{2,1,0:T(8,128)(2,1)}, u32[]{:S(2)}) copy-start(bf16[1,32,2560]{2,1,0:T(8,128)(2,1)} %param.9) | copy-start | bytes 491524
  10.3 97.8 %collective-permute-start = (bf16[1,64,1280]{2,1,0:T(8,128)(2,1)}, bf16[1,64,1280]{2,1,0:T(8,128)(2,1)}, u32[]{:S(2)}, u32[]{:S(2)}) collective-permute-start(bf16[1,64,1280]{2,1,0:T(8,128)(2,1)} %param.13), channel_id=1, source_target_pairs={{0,4},{4,8},{8,12},{12,0},{1,5},{5,9},{9,13},{13,1},{2,6},{6,10},{... | collective-permute-start | bytes 491528 | tf_op jit(solution)/shard_map/ppermute | solution.py:95
  13.4 95.1 %collective-permute-start.2 = (bf16[1,64,1280]{2,1,0:T(8,128)(2,1)}, bf16[1,64,1280]{2,1,0:T(8,128)(2,1)}, u32[]{:S(2)}, u32[]{:S(2)}) collective-permute-start(bf16[1,64,1280]{2,1,0:T(8,128)(2,1)} %param.13), channel_id=1, source_target_pairs={{4,0},{8,4},{12,8},{0,12},{5,1},{9,5},{13,9},{1,13},{6,2},{10,6},{... | collective-permute-start | bytes 491528 | tf_op jit(solution)/shard_map/ppermute | solution.py:97
  17.0 19.2 %copy-start = (bf16[1,512,1280]{2,1,0:T(8,128)(2,1)S(1)}, bf16[1,512,1280]{2,1,0:T(8,128)(2,1)}, u32[]{:S(2)}) copy-start(bf16[1,512,1280]{2,1,0:T(8,128)(2,1)} %param.16) | copy-start | bytes 3932164
  32.7 56.7 %all-to-all-start.1 = ((bf16[2,2,20480]{2,1,0:T(2,128)(2,1)}), bf16[2,2,20480]{2,1,0:T(2,128)(2,1)S(1)}, u32[]{:S(2)}, u32[]{:S(2)}) async-start(bf16[2,2,20480]{2,1,0:T(2,128)(2,1)} %reshape.165), calls=%async_computation.1 | async-start | bytes 327680 | tf_op jit(solution)/shard_map/all_to_all | solution.py:72
  36.2 96.9 %all-gather.5.cloned.1.call-start = ((), (), s32[]{:S(2)}) async-start(), calls=%async_computation.5 | async-start | bytes 3932160 | tf_op jit(solution)/shard_map/all_gather | solution.py:113
  38.3 0.9 copy-start.1
  38.3 1.0 copy-start.2
  38.4 17.9 %copy-start.4 = (bf16[1,32,2560]{2,1,0:T(8,128)(2,1)S(1)}, bf16[1,32,2560]{2,1,0:T(8,128)(2,1)}, u32[]{:S(2)}) copy-start(bf16[1,32,2560]{2,1,0:T(8,128)(2,1)} %param.10) | copy-start | bytes 491524
  57.2 15.7 %copy-start.5 = (bf16[1,32,2560]{2,1,0:T(8,128)(2,1)S(1)}, bf16[1,32,2560]{2,1,0:T(8,128)(2,1)}, u32[]{:S(2)}) copy-start(bf16[1,32,2560]{2,1,0:T(8,128)(2,1)} %param.11) | copy-start | bytes 491524
  89.4 8.1 %all-to-all-start = ((bf16[2,2,20480]{2,1,0:T(2,128)(2,1)}), bf16[2,2,20480]{2,1,0:T(2,128)(2,1)S(1)}, u32[]{:S(2)}, u32[]{:S(2)}) async-start(bf16[2,2,20480]{2,1,0:T(2,128)(2,1)} %reshape.163), calls=%async_computation | async-start | bytes 327680 | tf_op jit(solution)/shard_map/all_to_all | solution.py:73
  97.5 8.1 %all-to-all-start.2 = ((bf16[2,2,20480]{2,1,0:T(2,128)(2,1)}), bf16[2,2,20480]{2,1,0:T(2,128)(2,1)S(1)}, u32[]{:S(2)}, u32[]{:S(2)}) async-start(bf16[2,2,20480]{2,1,0:T(2,128)(2,1)} %reshape.167), calls=%async_computation.2 | async-start | bytes 327680 | tf_op jit(solution)/shard_map/all_to_all | solution.py:74
  101.2 6.6 %copy-start.6 = (pred[256]{0:T(512)(128)(4,1)}, pred[256]{0:T(512)(128)(4,1)S(1)}, u32[]{:S(2)}) copy-start(pred[256]{0:T(512)(128)(4,1)S(1)} %compare_or_fusion) | copy-start | bytes 772
  108.1 7.4 %collective-permute-start.1 = (bf16[1,64,1280]{2,1,0:T(8,128)(2,1)}, bf16[1,64,1280]{2,1,0:T(8,128)(2,1)S(1)}, u32[]{:S(2)}, u32[]{:S(2)}) collective-permute-start(bf16[1,64,1280]{2,1,0:T(8,128)(2,1)} %collective-permute-done), channel_id=1, source_target_pairs={{0,4},{4,8},{8,12},{12,0},{1,5},{5,9},{9,13},{13,1},{2,6},{6,10},{... | collective-permute-start | bytes 491528 | tf_op jit(solution)/shard_map/ppermute | solution.py:95
  117.2 0.7 copy-start.7
  118.3 6.0 %copy-start.8 = (s32[1,512]{1,0:T(1,128)S(1)}, s32[1,512]{1,0:T(1,128)}, u32[]{:S(2)}) copy-start(s32[1,512]{1,0:T(1,128)} %param.17) | copy-start | bytes 6148
  120.8 8.1 %all-to-all-start.3 = ((bf16[2,2,20480]{2,1,0:T(2,128)(2,1)}), bf16[2,2,20480]{2,1,0:T(2,128)(2,1)S(1)}, u32[]{:S(2)}, u32[]{:S(2)}) async-start(bf16[2,2,20480]{2,1,0:T(2,128)(2,1)} %reshape.169), calls=%async_computation.3 | async-start | bytes 327680 | tf_op jit(solution)/shard_map/all_to_all | solution.py:125
Sparse Core Ops, SparseCore 0:
  10.4 43.4 all-gather.2
  55.5 39.8 all-gather.4
